TPU v7x, 32 devices: a whole 2x2x4 slice. The times are simulated.
32 devices in a mesh: dp: 8 (over y, x, core), fsdp: 4 (over z).
Axes of the slice: x: 2, y: 2, z: 4, core: 2. Of those that a mesh axis runs over, the one named last changes fastest.
Arguments:
- patches: bfloat16 [2, 2048, 1152], P(None, ('dp', 'fsdp')), may hold values from -6 to 6
- cotangent: bfloat16 [2, 2048, 1152], P(None, ('dp', 'fsdp')), may hold values from -6 to 6
- conditioning: float32 [2, 8, 1152], replicated, may hold values from -6 to 6
- frame_of_slot: int32 [2, 2048], P(None, ('dp', 'fsdp')), may hold values from 0 to 127, as said below
- clip_of_slot: int32 [2, 2048], P(None, ('dp', 'fsdp')), may hold values from 0 to 7, as said below
- w_ada: bfloat16 [1152, 6912], P('dp', 'fsdp'), may hold values from -0.1875 to 0.1875
- b_ada: bfloat16 [6912], P('fsdp'), may hold values from -3 to 3
- w_qkv: bfloat16 [1152, 3456], P('dp', 'fsdp'), may hold values from -0.1875 to 0.1875
- b_qv: bfloat16 [2304], P('fsdp'), may hold values from -2 to 2
- w_proj: bfloat16 [1152, 1152], P('dp', 'fsdp'), may hold values from -1 to 1
- b_proj: bfloat16 [1152], P('fsdp'), may hold values from -2 to 2
- w_fc1: bfloat16 [1152, 4608], P('dp', 'fsdp'), may hold values from -0.1875 to 0.1875
- b_fc1: bfloat16 [4608], P('fsdp'), may hold values from -3 to 3
- w_fc2: bfloat16 [4608, 1152], P('dp', 'fsdp'), may hold values from -0.09375 to 0.09375
- b_fc2: bfloat16 [1152], P('fsdp'), may hold values from -2 to 2
Outputs:
- output: bfloat16 [2, 2048, 1152], P(None, ('dp', 'fsdp'))
- input_grad: bfloat16 [2, 2048, 1152], P(None, ('dp', 'fsdp'))
- cond_grad: float32 [2, 8, 1152], P(None, None, 'fsdp')
- grad_w_ada: float32 [1152, 6912], P('dp', 'fsdp')
- grad_b_ada: float32 [6912], P('fsdp')
- grad_w_qkv: float32 [1152, 3456], P('dp', 'fsdp')
- grad_b_qv: float32 [2304], P('fsdp')
- grad_w_proj: float32 [1152, 1152], P('dp', 'fsdp')
- grad_b_proj: float32 [1152], P('fsdp')
- grad_w_fc1: float32 [1152, 4608], P('dp', 'fsdp')
- grad_b_fc1: float32 [4608], P('fsdp')
- grad_w_fc2: float32 [4608, 1152], P('dp', 'fsdp')
- grad_b_fc2: float32 [1152], P('fsdp')
Inputs may be any that keep to these rules, and one draw needn't show every extreme that they name: `frame_of_slot`: in each micro-batch, each aligned block of 64 slots holds either one frame of 64 patches or four frames of 16 patches one after another; no frame number appears in two blocks. `clip_of_slot`: all slots of one frame name the same clip.
All inputs are finite; a program needn't handle non-finite values.
Results may differ from a plain program's by a relative error of at most 0.018.
Values may be sent and summed in bfloat16 or wider, within the bound.
A program may use at most 256 MiB of HBM per device.

v0:
```python
import math
import jax
import jax.numpy as jnp
from jax import lax
from jax.sharding import PartitionSpec as P

HEAD_DIM = 72
EPS = 1e-06
GELU_C = math.sqrt(2.0 / math.pi)
PRECISE = lax.Precision.HIGHEST
NEG_FILL = -1e30


def layer_norm(values):
    centre = values - jnp.mean(values, axis=-1, keepdims=True)
    return centre * lax.rsqrt(jnp.mean(centre * centre, axis=-1, keepdims=True) + EPS)


def gelu_tanh(hidden):
    return 0.5 * hidden * (1.0 + jnp.tanh(GELU_C * (hidden + 0.044715 * hidden * hidden * hidden)))


def modulate(values, shift_part, scale_part):
    return layer_norm(values) * (1.0 + scale_part) + shift_part


def matmul_plain(left, right):
    return jnp.dot(left, right, preferred_element_type=jnp.float32)


def matmul_right_t(left, right):
    return lax.dot_general(
        left, right, (((1,), (1,)), ((), ())), preferred_element_type=jnp.float32
    )


def matmul_left_t(left, right):
    return lax.dot_general(
        left, right, (((0,), (0,)), ((), ())), preferred_element_type=jnp.float32
    )


def precise_left_t(left, right):
    return lax.dot_general(
        left, right, (((0,), (0,)), ((), ())), precision=PRECISE, preferred_element_type=jnp.float32
    )


def precise_right_t(left, right):
    return lax.dot_general(
        left, right, (((1,), (1,)), ((), ())), precision=PRECISE, preferred_element_type=jnp.float32
    )


def gather_weights(w_qkv, w_proj, w_fc1, w_fc2, b_qv, b_proj, b_fc1, b_fc2):
    inner_parts = (
        lax.all_gather(w_qkv, "fsdp", axis=1, tiled=True),
        lax.all_gather(w_proj, "fsdp", axis=1, tiled=True),
        lax.all_gather(w_fc1, "fsdp", axis=1, tiled=True),
        lax.all_gather(w_fc2, "fsdp", axis=1, tiled=True),
        lax.all_gather(b_qv, "fsdp", axis=0, tiled=True),
        lax.all_gather(b_proj, "fsdp", axis=0, tiled=True),
        lax.all_gather(b_fc1, "fsdp", axis=0, tiled=True),
        lax.all_gather(b_fc2, "fsdp", axis=0, tiled=True),
    )
    whole_rows = (
        lax.all_gather(inner_parts[0], "dp", axis=0, tiled=True),
        lax.all_gather(inner_parts[1], "dp", axis=0, tiled=True),
        lax.all_gather(inner_parts[2], "dp", axis=0, tiled=True),
        lax.all_gather(inner_parts[3], "dp", axis=0, tiled=True),
    )
    return (
        whole_rows[0],
        whole_rows[1],
        whole_rows[2],
        whole_rows[3],
        inner_parts[4],
        inner_parts[5],
        inner_parts[6],
        inner_parts[7],
    )


def reduce_grads(full_w, full_b):
    inner_sums = (
        lax.psum_scatter(
            full_w[0].astype(jnp.bfloat16), "fsdp", scatter_dimension=1, tiled=True
        ).astype(jnp.float32),
        lax.psum_scatter(
            full_w[1].astype(jnp.bfloat16), "fsdp", scatter_dimension=1, tiled=True
        ).astype(jnp.float32),
        lax.psum_scatter(
            full_w[2].astype(jnp.bfloat16), "fsdp", scatter_dimension=1, tiled=True
        ).astype(jnp.float32),
        lax.psum_scatter(
            full_w[3].astype(jnp.bfloat16), "fsdp", scatter_dimension=1, tiled=True
        ).astype(jnp.float32),
        lax.psum_scatter(
            full_b[0].astype(jnp.bfloat16), "fsdp", scatter_dimension=0, tiled=True
        ).astype(jnp.float32),
        lax.psum_scatter(
            full_b[1].astype(jnp.bfloat16), "fsdp", scatter_dimension=0, tiled=True
        ).astype(jnp.float32),
        lax.psum_scatter(
            full_b[2].astype(jnp.bfloat16), "fsdp", scatter_dimension=0, tiled=True
        ).astype(jnp.float32),
        lax.psum_scatter(
            full_b[3].astype(jnp.bfloat16), "fsdp", scatter_dimension=0, tiled=True
        ).astype(jnp.float32),
    )
    outer_sums = (
        lax.psum_scatter(
            inner_sums[0].astype(jnp.bfloat16), "dp", scatter_dimension=0, tiled=True
        ).astype(jnp.float32),
        lax.psum_scatter(
            inner_sums[1].astype(jnp.bfloat16), "dp", scatter_dimension=0, tiled=True
        ).astype(jnp.float32),
        lax.psum_scatter(
            inner_sums[2].astype(jnp.bfloat16), "dp", scatter_dimension=0, tiled=True
        ).astype(jnp.float32),
        lax.psum_scatter(
            inner_sums[3].astype(jnp.bfloat16), "dp", scatter_dimension=0, tiled=True
        ).astype(jnp.float32),
    )
    small_sums = lax.psum((inner_sums[4], inner_sums[5], inner_sums[6], inner_sums[7]), "dp")
    return (tuple(outer_sums), tuple(small_sums))


def modulation_sharded(silu_low, w_ada, b_ada):
    row_width, col_width = w_ada.shape
    row_start = lax.axis_index("dp") * row_width
    col_start = lax.axis_index("fsdp") * col_width
    silu_part = lax.dynamic_slice_in_dim(silu_low, row_start, row_width, 1)
    partial_value = matmul_plain(silu_part, w_ada)
    bias_term = jnp.where(
        lax.axis_index("dp") == 0, b_ada.astype(jnp.float32), jnp.zeros((col_width,), jnp.float32)
    )
    partial_value = partial_value + bias_term[None, :]
    padded = jnp.zeros((silu_low.shape[0], col_width * lax.axis_size("fsdp")), jnp.float32)
    padded = lax.dynamic_update_slice_in_dim(padded, partial_value, col_start, 1)
    return lax.psum(padded, ("dp", "fsdp"))


def ada_grads_sharded(silu_low, cond_rows, d_modulation, w_ada):
    row_width, col_width = w_ada.shape
    row_start = lax.axis_index("dp") * row_width
    col_start = lax.axis_index("fsdp") * col_width
    d_total = lax.psum(d_modulation, ("dp", "fsdp"))
    d_cols = lax.dynamic_slice_in_dim(d_total, col_start, col_width, 1)
    silu_part = lax.dynamic_slice_in_dim(silu_low, row_start, row_width, 1).astype(jnp.float32)
    grad_weight = precise_left_t(silu_part, d_cols)
    grad_bias = jnp.sum(d_cols, axis=0)
    d_silu_part = precise_right_t(d_cols, w_ada.astype(jnp.float32))
    model_width = cond_rows.shape[1]
    padded = jnp.zeros((cond_rows.shape[0], model_width), jnp.float32)
    padded = lax.dynamic_update_slice_in_dim(padded, d_silu_part, row_start, 1)
    d_silu = lax.psum(padded, ("dp", "fsdp"))
    own_width = model_width // lax.axis_size("fsdp")
    own_start = lax.axis_index("fsdp") * own_width
    d_silu_own = lax.dynamic_slice_in_dim(d_silu, own_start, own_width, 1)
    cond_own = lax.dynamic_slice_in_dim(cond_rows, own_start, own_width, 1)
    silu_own, silu_own_back = jax.vjp(jax.nn.silu, cond_own)
    cond_grad = silu_own_back(d_silu_own)[0]
    return (grad_weight, grad_bias, cond_grad)


def head_scores(queries, key_rows, same_frame):
    scores = jnp.einsum(
        "qhd,khd->hqk", queries, key_rows, preferred_element_type=jnp.float32
    ) * HEAD_DIM ** (-0.5)
    return jnp.where(same_frame[None, :, :], scores, NEG_FILL)


def micro_forward(patch_rows, modulation, frame_ids, clip_ids, weights):
    w_qkv, w_proj, w_fc1, w_fc2, b_qv, b_proj, b_fc1, b_fc2 = weights
    row_count, model_width = patch_rows.shape
    head_count = model_width // HEAD_DIM
    clip_hot = (
        clip_ids[:, None] == jnp.arange(modulation.shape[0], dtype=jnp.int32)[None, :]
    ).astype(jnp.float32)
    token_mod = jnp.dot(clip_hot, modulation, precision=PRECISE)
    shift_one, scale_one, gate_one, shift_two, scale_two, gate_two = jnp.split(token_mod, 6, axis=1)
    inputs_float = patch_rows.astype(jnp.float32)
    attn_in, norm_one_back = jax.vjp(modulate, inputs_float, shift_one, scale_one)
    attn_low = attn_in.astype(jnp.bfloat16)
    qkv_bias = jnp.concatenate(
        [b_qv[:model_width], jnp.zeros((model_width,), jnp.bfloat16), b_qv[model_width:]]
    ).astype(jnp.float32)
    qkv_low = (matmul_plain(attn_low, w_qkv) + qkv_bias).astype(jnp.bfloat16)
    queries = qkv_low[:, :model_width].reshape(row_count, head_count, HEAD_DIM)
    key_rows = qkv_low[:, model_width : 2 * model_width].reshape(row_count, head_count, HEAD_DIM)
    value_rows = qkv_low[:, 2 * model_width :].reshape(row_count, head_count, HEAD_DIM)
    same_frame = frame_ids[:, None] == frame_ids[None, :]
    scores = head_scores(queries, key_rows, same_frame)
    row_max = jnp.max(scores, axis=-1, keepdims=True)
    exp_scores = jnp.exp(scores - row_max)
    exp_total = jnp.sum(exp_scores, axis=-1, keepdims=True)
    shares = exp_scores / exp_total
    log_total = row_max + jnp.log(exp_total)
    mixed_low = (
        jnp.einsum(
            "hqk,khd->qhd",
            shares.astype(jnp.bfloat16),
            value_rows,
            preferred_element_type=jnp.float32,
        )
        .reshape(row_count, model_width)
        .astype(jnp.bfloat16)
    )
    attn_out = matmul_plain(mixed_low, w_proj) + b_proj.astype(jnp.float32)
    after_attn = inputs_float + gate_one * attn_out
    mlp_in, norm_two_back = jax.vjp(modulate, after_attn, shift_two, scale_two)
    mlp_low = mlp_in.astype(jnp.bfloat16)
    hidden = matmul_plain(mlp_low, w_fc1) + b_fc1.astype(jnp.float32)
    act_value, gelu_back = jax.vjp(gelu_tanh, hidden)
    act_low = act_value.astype(jnp.bfloat16)
    branch = matmul_plain(act_low, w_fc2) + b_fc2.astype(jnp.float32)
    output = (after_attn + gate_two * branch).astype(jnp.bfloat16)
    saved = (
        clip_hot,
        gate_one,
        gate_two,
        norm_one_back,
        attn_low,
        queries,
        key_rows,
        value_rows,
        same_frame,
        log_total,
        mixed_low,
        attn_out,
        norm_two_back,
        mlp_low,
        gelu_back,
        act_low,
        branch,
    )
    return (output, saved)


def micro_backward(saved, cot_rows, weights):
    w_qkv, w_proj, w_fc1, w_fc2 = (weights[0], weights[1], weights[2], weights[3])
    (
        clip_hot,
        gate_one,
        gate_two,
        norm_one_back,
        attn_low,
        queries,
        key_rows,
        value_rows,
        same_frame,
        log_total,
        mixed_low,
        attn_out,
        norm_two_back,
        mlp_low,
        gelu_back,
        act_low,
        branch,
    ) = saved
    row_count = cot_rows.shape[0]
    model_width = cot_rows.shape[1]
    head_count = model_width // HEAD_DIM
    cot_float = cot_rows.astype(jnp.float32)
    d_branch = (gate_two * cot_float).astype(jnp.bfloat16)
    grad_gate_two = cot_float * branch
    grad_w_fc2 = matmul_left_t(act_low, d_branch)
    grad_b_fc2 = jnp.sum(d_branch.astype(jnp.float32), axis=0)
    d_act = matmul_right_t(d_branch, w_fc2)
    d_hidden = gelu_back(d_act)[0].astype(jnp.bfloat16)
    grad_w_fc1 = matmul_left_t(mlp_low, d_hidden)
    grad_b_fc1 = jnp.sum(d_hidden.astype(jnp.float32), axis=0)
    d_mlp = matmul_right_t(d_hidden, w_fc1)
    d_after, d_shift_two, d_scale_two = norm_two_back(d_mlp)
    d_after = cot_float + d_after
    grad_gate_one = d_after * attn_out
    d_attn = (gate_one * d_after).astype(jnp.bfloat16)
    grad_w_proj = matmul_left_t(mixed_low, d_attn)
    grad_b_proj = jnp.sum(d_attn.astype(jnp.float32), axis=0)
    d_mix = (
        matmul_right_t(d_attn, w_proj).astype(jnp.bfloat16).reshape(row_count, head_count, HEAD_DIM)
    )
    shares_again = jnp.exp(head_scores(queries, key_rows, same_frame) - log_total)
    d_shares = jnp.einsum("qhd,khd->hqk", d_mix, value_rows, preferred_element_type=jnp.float32)
    row_delta = jnp.sum(shares_again * d_shares, axis=-1, keepdims=True)
    d_scores = (shares_again * (d_shares - row_delta)).astype(jnp.bfloat16)
    d_queries = jnp.einsum(
        "hqk,khd->qhd", d_scores, key_rows, preferred_element_type=jnp.float32
    ) * HEAD_DIM ** (-0.5)
    d_keys = jnp.einsum(
        "hqk,qhd->khd", d_scores, queries, preferred_element_type=jnp.float32
    ) * HEAD_DIM ** (-0.5)
    d_values = jnp.einsum(
        "hqk,qhd->khd", shares_again.astype(jnp.bfloat16), d_mix, preferred_element_type=jnp.float32
    )
    d_qkv = jnp.concatenate(
        [
            d_queries.reshape(row_count, model_width),
            d_keys.reshape(row_count, model_width),
            d_values.reshape(row_count, model_width),
        ],
        axis=1,
    ).astype(jnp.bfloat16)
    grad_w_qkv = matmul_left_t(attn_low, d_qkv)
    column_sums = jnp.sum(d_qkv.astype(jnp.float32), axis=0)
    grad_b_qv = jnp.concatenate([column_sums[:model_width], column_sums[2 * model_width :]])
    d_attn_in = matmul_right_t(d_qkv, w_qkv)
    d_inputs, d_shift_one, d_scale_one = norm_one_back(d_attn_in)
    input_grad = (d_after + d_inputs).astype(jnp.bfloat16)
    d_token_mod = jnp.concatenate(
        [d_shift_one, d_scale_one, grad_gate_one, d_shift_two, d_scale_two, grad_gate_two], axis=1
    )
    d_modulation = lax.dot_general(
        clip_hot,
        d_token_mod,
        (((0,), (0,)), ((), ())),
        precision=PRECISE,
        preferred_element_type=jnp.float32,
    )
    grads_w = (grad_w_qkv, grad_w_proj, grad_w_fc1, grad_w_fc2)
    grads_b = (grad_b_qv, grad_b_proj, grad_b_fc1, grad_b_fc2)
    return (input_grad, d_modulation, grads_w, grads_b)


def add_terms(first_terms, second_terms):
    if first_terms is None:
        return tuple(second_terms)
    return tuple(
        (first_item + second_item for first_item, second_item in zip(first_terms, second_terms))
    )


def per_device(
    patches,
    cotangent,
    conditioning,
    frame_of_slot,
    clip_of_slot,
    w_ada,
    b_ada,
    w_qkv,
    b_qv,
    w_proj,
    b_proj,
    w_fc1,
    b_fc1,
    w_fc2,
    b_fc2,
):
    micro_count = patches.shape[0]
    outputs = []
    input_grads = []
    cond_parts = []
    summed_w = None
    summed_b = None
    ada_terms = None
    for micro_index in range(micro_count):
        cond_rows = conditioning[micro_index]
        silu_value, silu_back = jax.vjp(jax.nn.silu, cond_rows)
        silu_low = silu_value.astype(jnp.bfloat16)
        weights = gather_weights(w_qkv, w_proj, w_fc1, w_fc2, b_qv, b_proj, b_fc1, b_fc2)
        modulation = modulation_sharded(silu_low, w_ada, b_ada)
        output, saved = micro_forward(
            patches[micro_index],
            modulation,
            frame_of_slot[micro_index],
            clip_of_slot[micro_index],
            weights,
        )
        input_grad, d_modulation, grads_w, grads_b = micro_backward(
            saved, cotangent[micro_index], weights
        )
        outputs.append(output)
        input_grads.append(input_grad)
        grad_w_ada, grad_b_ada, cond_grad = ada_grads_sharded(
            silu_low, cond_rows, d_modulation, w_ada
        )
        cond_parts.append(cond_grad[None])
        ada_terms = add_terms(ada_terms, (grad_w_ada, grad_b_ada))
        part_w, part_b = reduce_grads(grads_w, grads_b)
        summed_w = add_terms(summed_w, part_w)
        summed_b = add_terms(summed_b, part_b)
    cond_all = jnp.concatenate(cond_parts, axis=0)
    return (
        jnp.stack(outputs),
        jnp.stack(input_grads),
        cond_all,
        ada_terms[0],
        ada_terms[1],
        summed_w[0],
        summed_b[0],
        summed_w[1],
        summed_b[1],
        summed_w[2],
        summed_b[2],
        summed_w[3],
        summed_b[3],
    )


def solution(mesh):
    in_specs = (
        P(None, ("dp", "fsdp"), None),
        P(None, ("dp", "fsdp"), None),
        P(),
        P(None, ("dp", "fsdp")),
        P(None, ("dp", "fsdp")),
        P("dp", "fsdp"),
        P("fsdp"),
        P("dp", "fsdp"),
        P("fsdp"),
        P("dp", "fsdp"),
        P("fsdp"),
        P("dp", "fsdp"),
        P("fsdp"),
        P("dp", "fsdp"),
        P("fsdp"),
    )
    out_specs = (
        P(None, ("dp", "fsdp"), None),
        P(None, ("dp", "fsdp"), None),
        P(None, None, "fsdp"),
        P("dp", "fsdp"),
        P("fsdp"),
        P("dp", "fsdp"),
        P("fsdp"),
        P("dp", "fsdp"),
        P("fsdp"),
        P("dp", "fsdp"),
        P("fsdp"),
        P("dp", "fsdp"),
        P("fsdp"),
    )
    return jax.shard_map(
        per_device, mesh=mesh, in_specs=in_specs, out_specs=out_specs, check_vma=False
    )
```

profile of v0, /device:TPU:0, one launch (start us, length us, event | category | flops | bytes accessed | tf_op | source)
XLA Modules:
  0.0 1921.0 jit_solution(4469489425580298956)
XLA Ops:
  14.6 38.8 %all-gather = bf16[4,864,144]{1,2,0:T(8,128)(2,1)S(1)} all-gather(bf16[1,864,144]{1,2,0:T(8,128)(2,1)S(1)} %bitcast.245), channel_id=1, replica_groups=mesh['dp'=8,'fsdp'=4] {'fsdp'}, dimensions={0}, use_global_device_ids=true | all-gather | bytes 1244160 | tf_op jit(solution)/shard_map/all_gather | solution.py:57
  55.6 15.8 all-gather.1
  73.3 24.5 %all-gather.18.cloned.1.call-done = bf16[576,1152]{0,1:T(8,128)(2,1)} async-done(((bf16[576,288]{0,1:T(8,128)(2,1)}), bf16[576,1152]{0,1:T(8,128)(2,1)}) %all-gather.18.cloned.1.call-update) | async-done | bytes 1327120 | tf_op jit(solution)/shard_map/all_gather | solution.py:60
  102.9 16.8 all-reduce.16
  119.7 13.1 all-gather.2
  135.2 69.7 %all-reduce.25.cloned.1.call-done = (f32[8,6912]{1,0:T(8,128)}, f32[8,6912]{1,0:T(8,128)}) async-done(((f32[8,6912]{1,0:T(8,128)}, f32[8,6912]{1,0:T(8,128)}), (f32[8,6912]{1,0:T(8,128)}, f32[8,6912]{1,0:T(8,128)})) %all-reduce.25.cloned.1.call-update) | async-done | bytes 442384 | tf_op jit(solution)/shard_map/psum | solution.py:141
  209.6 4.7 fusion.1
  217.8 6.2 fusion
  228.0 2.6 convolution_add_fusion.5
  230.7 2.8 fusion.146
  238.5 12.5 all-gather.16.cloned.1.call-done
  251.0 7.1 convolution_add_fusion.1
  258.2 58.6 %all-gather.20.cloned.1.call-done = bf16[4608,1152]{1,0:T(8,128)(2,1)} async-done(((bf16[576,1152]{1,0:T(8,128)(2,1)}), bf16[4608,1152]{1,0:T(8,128)(2,1)}) %all-gather.20.cloned.1.call-update) | async-done | bytes 10616848 | tf_op jit(solution)/shard_map/all_gather | solution.py:70
  316.8 8.8 fusion.139
  325.6 3.4 multiply_reduce_fusion.3
  331.1 8.6 fusion.141
  339.7 3.4 multiply_reduce_fusion.2
  363.6 6.0 fusion.160
  369.7 7.6 fusion.55
  378.1 20.2 %all-reduce.15 = (bf16[1152]{0:T(1024)(128)(2,1)S(1)}, bf16[2304]{0:T(1024)(128)(2,1)}, bf16[2304]{0:T(1024)(128)(2,1)}, bf16[1152]{0:T(1024)(128)(2,1)}, bf16[1...) all-reduce(bf16[1152]{0:T(1024)(128)(2,1)S(1)} %copy-done.101, ...), channel_id=1, replica_groups=mesh['dp'=8,'fsdp'=4] {'fsdp'}, use_global_device_ids=true, to_apply=%add.2 | all-reduce | flops 19584 | bytes 78336
  399.2 6.5 convolution_add_fusion.7
  424.7 5.4 convolution_convert_fusion.4
  431.1 5.4 convolution_convert_fusion.5
  437.4 5.6 convolution_convert_fusion
  444.0 5.6 convolution_convert_fusion.1
  450.6 5.5 convolution_convert_fusion.2
  456.2 14.8 copy.162
  472.1 5.5 convolution_convert_fusion.3
  477.7 15.3 copy.160
  493.1 315.4 %all-reduce.23.cloned.1.call-done = (f32[8,6912]{1,0:T(8,128)}, f32[8,6912]{1,0:T(8,128)}) async-done(((f32[8,6912]{1,0:T(8,128)}, f32[8,6912]{1,0:T(8,128)}), (f32[8,6912]{1,0:T(8,128)}, f32[8,6912]{1,0:T(8,128)})) %all-reduce.23.cloned.1.call-update) | async-done | bytes 442384 | tf_op jit(solution)/shard_map/psum | solution.py:148
  817.4 4.1 copy.154
  821.7 4.1 copy.152
  825.8 168.8 %reduce-scatter.47.cloned.1.call-done = bf16[4608,288]{0,1:T(8,128)(2,1)} async-done(((bf16[4608,1152]{0,1:T(8,128)(2,1)}), bf16[4608,288]{0,1:T(8,128)(2,1)}) %reduce-scatter.47.cloned.1.call-update) | async-done | bytes 2654224 | tf_op jit(solution)/shard_map/reduce_scatter | solution.py:95
  994.7 4.7 copy.166
  999.5 179.6 %reduce-scatter.45.cloned.1.call-done = bf16[4608,288]{0,1:T(8,128)(2,1)} async-done(((bf16[4608,1152]{0,1:T(8,128)(2,1)}), bf16[4608,288]{0,1:T(8,128)(2,1)}) %reduce-scatter.45.cloned.1.call-update) | async-done | bytes 2654224 | tf_op jit(solution)/shard_map/reduce_scatter | solution.py:95
  1179.0 4.7 copy.164
  1183.8 179.3 %reduce-scatter.59.cloned.1.call-done = bf16[1152,1152]{1,0:T(8,128)(2,1)} async-done(((bf16[4608,1152]{1,0:T(8,128)(2,1)}), bf16[1152,1152]{1,0:T(8,128)(2,1)}) %reduce-scatter.59.cloned.1.call-update) | async-done | bytes 2654224
  1363.2 5.2 copy.163
  1368.5 178.4 %reduce-scatter.57.cloned.1.call-done = bf16[1152,1152]{1,0:T(8,128)(2,1)} async-done(((bf16[4608,1152]{1,0:T(8,128)(2,1)}), bf16[1152,1152]{1,0:T(8,128)(2,1)}) %reduce-scatter.57.cloned.1.call-update) | async-done | bytes 2654224
  1546.9 5.2 copy.161
  1557.3 24.7 %all-reduce.14 = (f32[576]{0:T(1024)}, f32[288]{0:T(512)}, f32[1152]{0:T(1024)}, f32[288]{0:T(512)}) all-reduce(f32[576]{0:T(1024)S(1)} %convert_add_fusion.7, f32[288]{0:T(512)S(1)} %convert_add_fusion.9, f32[1152]{0:T(1024)S(1)} %convert_add_fusion.6, f32[288]{0:T(512)S(1)} %convert_add_fusion.8), channel_id=1, replica_groups=mesh['dp'=8,'fsdp'=4] {'dp'}, use_global_device_ids=true, to_apply=%region_36.37 | all-reduce | flops 2304 | bytes 18432 | tf_op jit(solution)/shard_map/psum | solution.py:125
  1590.9 33.9 %reduce-scatter.53.cloned.1.call-done = bf16[144,288]{1,0:T(8,128)(2,1)} async-done(((bf16[1152,288]{1,0:T(8,128)(2,1)}), bf16[144,288]{1,0:T(8,128)(2,1)}) %reduce-scatter.53.cloned.1.call-update) | async-done | bytes 82960
  1626.6 42.2 %reduce-scatter.51.cloned.1.call-done = bf16[144,864]{1,0:T(8,128)(2,1)} async-done(((bf16[1152,864]{1,0:T(8,128)(2,1)}), bf16[144,864]{1,0:T(8,128)(2,1)}) %reduce-scatter.51.cloned.1.call-update) | async-done | bytes 248848
  1669.9 43.3 %reduce-scatter.49.cloned.1.call-done = bf16[144,864]{1,0:T(8,128)(2,1)} async-done(((bf16[1152,864]{1,0:T(8,128)(2,1)}), bf16[144,864]{1,0:T(8,128)(2,1)}) %reduce-scatter.49.cloned.1.call-update) | async-done | bytes 248848
  1715.6 49.3 %reduce-scatter.63.cloned.1.call-done = bf16[576,288]{1,0:T(8,128)(2,1)} async-done(((bf16[4608,288]{1,0:T(8,128)(2,1)}), bf16[576,288]{1,0:T(8,128)(2,1)}) %reduce-scatter.63.cloned.1.call-update) | async-done | bytes 331792
  1766.1 50.2 %reduce-scatter.61.cloned.1.call-done = bf16[576,288]{1,0:T(8,128)(2,1)} async-done(((bf16[4608,288]{1,0:T(8,128)(2,1)}), bf16[576,288]{1,0:T(8,128)(2,1)}) %reduce-scatter.61.cloned.1.call-update) | async-done | bytes 331792
  1818.5 45.1 %reduce-scatter.43.cloned.1.call-done = bf16[144,1152]{1,0:T(8,128)(2,1)} async-done(((bf16[1152,1152]{1,0:T(8,128)(2,1)}), bf16[144,1152]{1,0:T(8,128)(2,1)}) %reduce-scatter.43.cloned.1.call-update) | async-done | bytes 331792 | tf_op jit(solution)/shard_map/reduce_scatter | solution.py:118
  1863.5 47.7 %reduce-scatter.41.cloned.1.call-done = bf16[144,1152]{1,0:T(8,128)(2,1)} async-done(((bf16[1152,1152]{1,0:T(8,128)(2,1)}), bf16[144,1152]{1,0:T(8,128)(2,1)}) %reduce-scatter.41.cloned.1.call-update) | async-done | bytes 331792 | tf_op jit(solution)/shard_map/reduce_scatter | solution.py:118
  (523 shorter events, 112.1 us)
Async XLA Ops:
  8.0 64.7 %all-gather.14.cloned.1.call-start = ((), (), s32[]{:S(2)}) async-start(), calls=%async_computation.18 | async-start | bytes 1658880 | tf_op jit(solution)/shard_map/all_gather | solution.py:59
  8.8 89.0 %all-gather.18.cloned.1.call-start = ((), (), s32[]{:S(2)}) async-start(), calls=%async_computation.20 | async-start | bytes 1843200 | tf_op jit(solution)/shard_map/all_gather | solution.py:60
  9.5 195.4 %all-reduce.25.cloned.1.call-start = ((), (), s32[]{:S(2)}) async-start(), calls=%async_computation.40 | async-start | bytes 884736 | tf_op jit(solution)/shard_map/psum | solution.py:141
  14.6 195.0 %all-gather.10.cloned.1.call-start = ((), (), s32[]{:S(2)}) async-start(), calls=%async_computation.16 | async-start | bytes 8957952 | tf_op jit(solution)/shard_map/all_gather | solution.py:67
  55.6 172.4 %all-gather.12.cloned.1.call-start = ((), (), s32[]{:S(2)}) async-start(), calls=%async_computation.17 | async-start | bytes 2985984 | tf_op jit(solution)/shard_map/all_gather | solution.py:68
  72.6 178.4 %all-gather.16.cloned.1.call-start = ((), (), s32[]{:S(2)}) async-start(), calls=%async_computation.19 | async-start | bytes 11943936 | tf_op jit(solution)/shard_map/all_gather | solution.py:69
  73.2 27.3 %copy-start.125 = (u32[32]{0:T(128)S(1)}, u32[32]{0:T(128)}, u32[]{:S(2)}) copy-start(u32[32]{0:T(128)} %constant.84) | copy-start | bytes 388
  73.2 29.2 %copy-start.126 = (bf16[576]{0:T(1024)(128)(2,1)S(1)}, bf16[576]{0:T(1024)(128)(2,1)}, u32[]{:S(2)}) copy-start(bf16[576]{0:T(1024)(128)(2,1)} %param.23) | copy-start | bytes 3460
  73.2 29.4 %copy-start.133 = (bf16[288]{0:T(512)(128)(2,1)S(1)}, bf16[288]{0:T(512)(128)(2,1)}, u32[]{:S(2)}) copy-start(bf16[288]{0:T(512)(128)(2,1)} %param.25) | copy-start | bytes 1732
  73.3 46.4 %copy-start.122 = (bf16[1152]{0:T(1024)(128)(2,1)S(1)}, bf16[1152]{0:T(1024)(128)(2,1)}, u32[]{:S(2)}) copy-start(bf16[1152]{0:T(1024)(128)(2,1)} %param.27) | copy-start | bytes 6916
  73.3 59.7 %copy-start.134 = (bf16[288]{0:T(512)(128)(2,1)S(1)}, bf16[288]{0:T(512)(128)(2,1)}, u32[]{:S(2)}) copy-start(bf16[288]{0:T(512)(128)(2,1)} %param.29) | copy-start | bytes 1732
  73.3 60.7 %copy-start.17 = (bf16[2,64,1152]{2,1,0:T(8,128)(2,1)S(1)}, bf16[2,64,1152]{2,1,0:T(8,128)(2,1)}, u32[]{:S(2)}) copy-start(bf16[2,64,1152]{2,1,0:T(8,128)(2,1)} %param.15) | copy-start | bytes 884740
  73.3 243.5 %all-gather.20.cloned.1.call-start = ((), (), s32[]{:S(2)}) async-start(), calls=%async_computation.21 | async-start | bytes 11943936 | tf_op jit(solution)/shard_map/all_gather | solution.py:70
  100.4 34.6 %copy-start.135 = (s32[2,64]{1,0:T(2,128)S(1)}, s32[2,64]{1,0:T(2,128)}, u32[]{:S(2)}) copy-start(s32[2,64]{1,0:T(2,128)} %param.19) | copy-start | bytes 1540
  100.4 34.6 %copy-start.136 = (s32[2,64]{1,0:T(2,128)S(1)}, s32[2,64]{1,0:T(2,128)}, u32[]{:S(2)}) copy-start(s32[2,64]{1,0:T(2,128)} %param.18) | copy-start | bytes 1540
  100.4 708.0 %all-reduce.23.cloned.1.call-start = ((), (), s32[]{:S(2)}) async-start(), calls=%async_computation.39 | async-start | bytes 884736 | tf_op jit(solution)/shard_map/psum | solution.py:148
  134.1 75.1 %copy-start.106 = (f32[64]{0:T(128)}, f32[64]{0:T(128)S(1)}, u32[]{:S(2)}) copy-start(f32[64]{0:T(128)S(1)} %broadcast_multiply_fusion.3) | copy-start | bytes 772
  134.1 75.1 %copy-start.109 = (f32[64]{0:T(128)}, f32[64]{0:T(128)S(1)}, u32[]{:S(2)}) copy-start(f32[64]{0:T(128)S(1)} %broadcast_multiply_fusion.1) | copy-start | bytes 772
  134.9 74.3 %copy-start.129 = (f32[64]{0:T(128)}, f32[64]{0:T(128)S(1)}, u32[]{:S(2)}) copy-start(f32[64]{0:T(128)S(1)} %fusion.129) | copy-start | bytes 772
  135.0 74.3 %copy-start.131 = (f32[64]{0:T(128)}, f32[64]{0:T(128)S(1)}, u32[]{:S(2)}) copy-start(f32[64]{0:T(128)S(1)} %fusion.131) | copy-start | bytes 772
  135.0 72.7 %copy-start.118 = (s32[64]{0:T(128)}, s32[64]{0:T(128)S(1)}, u32[]{:S(2)}) copy-start(s32[64]{0:T(128)S(1)} %get-tuple-element.151) | copy-start | bytes 772
  135.0 72.7 %copy-start.120 = (s32[64]{0:T(128)}, s32[64]{0:T(128)S(1)}, u32[]{:S(2)}) copy-start(s32[64]{0:T(128)S(1)} %get-tuple-element.152) | copy-start | bytes 772
  363.5 14.4 copy-start.20
  363.5 14.4 copy-start.22
  369.7 29.4 %copy-start.5 = (f32[64,4608]{1,0:T(8,128)S(1)}, f32[64,4608]{1,0:T(8,128)}, u32[]{:S(2)}) copy-start(f32[64,4608]{1,0:T(8,128)} %copy-done.4) | copy-start | bytes 3538948
  417.3 395.2 %reduce-scatter.39.cloned.1.call-start = ((), (), s32[]{:S(2)}) async-start(), calls=%async_computation.25 | async-start | bytes 3317760 | tf_op jit(solution)/shard_map/reduce_scatter | solution.py:89
  420.1 394.8 %reduce-scatter.37.cloned.1.call-start = ((), (), s32[]{:S(2)}) async-start(), calls=%async_computation.24 | async-start | bytes 3317760 | tf_op jit(solution)/shard_map/reduce_scatter | solution.py:89
  423.5 393.9 %reduce-scatter.35.cloned.1.call-start = ((), (), s32[]{:S(2)}) async-start(), calls=%async_computation.23 | async-start | bytes 9953280 | tf_op jit(solution)/shard_map/reduce_scatter | solution.py:86
  430.1 391.6 %reduce-scatter.33.cloned.1.call-start = ((), (), s32[]{:S(2)}) async-start(), calls=%async_computation.22 | async-start | bytes 9953280 | tf_op jit(solution)/shard_map/reduce_scatter | solution.py:86
  436.5 558.1 %reduce-scatter.47.cloned.1.call-start = ((), (), s32[]{:S(2)}) async-start(), calls=%async_computation.29 | async-start | bytes 13271040 | tf_op jit(solution)/shard_map/reduce_scatter | solution.py:95
  443.1 735.9 %reduce-scatter.45.cloned.1.call-start = ((), (), s32[]{:S(2)}) async-start(), calls=%async_computation.28 | async-start | bytes 13271040 | tf_op jit(solution)/shard_map/reduce_scatter | solution.py:95
  449.6 913.6 %reduce-scatter.59.cloned.1.call-start = ((), (), s32[]{:S(2)}) async-start(), calls=%async_computation.35 | async-start | bytes 13271040
  471.0 1075.9 %reduce-scatter.57.cloned.1.call-start = ((), (), s32[]{:S(2)}) async-start(), calls=%async_computation.34 | async-start | bytes 13271040
  493.0 1094.6 %all-reduce.21.cloned.1.call-start = ((), (), s32[]{:S(2)}) async-start(), calls=%async_computation.38 | async-start | bytes 147456 | tf_op jit(solution)/shard_map/psum | solution.py:157
  812.5 777.4 %reduce-scatter.55.cloned.1.call-start = ((), (), s32[]{:S(2)}) async-start(), calls=%async_computation.33 | async-start | bytes 995328
  814.9 809.8 %reduce-scatter.53.cloned.1.call-start = ((), (), s32[]{:S(2)}) async-start(), calls=%async_computation.32 | async-start | bytes 995328
  817.4 851.4 %reduce-scatter.51.cloned.1.call-start = ((), (), s32[]{:S(2)}) async-start(), calls=%async_computation.31 | async-start | bytes 2322432
  821.6 891.6 %reduce-scatter.49.cloned.1.call-start = ((), (), s32[]{:S(2)}) async-start(), calls=%async_computation.30 | async-start | bytes 2322432
  825.8 939.0 %reduce-scatter.63.cloned.1.call-start = ((), (), s32[]{:S(2)}) async-start(), calls=%async_computation.37 | async-start | bytes 3981312
  999.4 816.9 %reduce-scatter.61.cloned.1.call-start = ((), (), s32[]{:S(2)}) async-start(), calls=%async_computation.36 | async-start | bytes 3981312
  1183.8 679.8 %reduce-scatter.43.cloned.1.call-start = ((), (), s32[]{:S(2)}) async-start(), calls=%async_computation.27 | async-start | bytes 2985984 | tf_op jit(solution)/shard_map/reduce_scatter | solution.py:118
  1368.4 542.8 %reduce-scatter.41.cloned.1.call-start = ((), (), s32[]{:S(2)}) async-start(), calls=%async_computation.26 | async-start | bytes 2985984 | tf_op jit(solution)/shard_map/reduce_scatter | solution.py:118
  1552.1 29.9 %copy-start.83 = (bf16[1,64,1152]{2,1,0:T(8,128)(2,1)S(1)}, bf16[1,64,1152]{2,1,0:T(8,128)(2,1)}, u32[]{:S(2)}) copy-start(bf16[1,64,1152]{2,1,0:T(8,128)(2,1)} %get-tuple-element.117) | copy-start | bytes 442372
  1552.1 29.9 %copy-start.84 = (bf16[1,64,1152]{2,1,0:T(8,128)(2,1)S(1)}, bf16[1,64,1152]{2,1,0:T(8,128)(2,1)}, u32[]{:S(2)}) copy-start(bf16[1,64,1152]{2,1,0:T(8,128)(2,1)} %get-tuple-element.116) | copy-start | bytes 442372
  1552.1 30.7 %copy-start.82 = (bf16[1,64,1152]{2,1,0:T(8,128)(2,1)S(1)}, bf16[1,64,1152]{2,1,0:T(8,128)(2,1)}, u32[]{:S(2)}) copy-start(bf16[1,64,1152]{2,1,0:T(8,128)(2,1)} %get-tuple-element.121) | copy-start | bytes 442372
  1552.1 30.7 %copy-start.85 = (bf16[1,64,1152]{2,1,0:T(8,128)(2,1)S(1)}, bf16[1,64,1152]{2,1,0:T(8,128)(2,1)}, u32[]{:S(2)}) copy-start(bf16[1,64,1152]{2,1,0:T(8,128)(2,1)} %get-tuple-element.123) | copy-start | bytes 442372
  1552.1 31.4 %copy-start.90 = (f32[8,6912]{1,0:T(8,128)S(1)}, f32[8,6912]{1,0:T(8,128)}, u32[]{:S(2)}) copy-start(f32[8,6912]{1,0:T(8,128)} %get-tuple-element.74) | copy-start | bytes 663556
  1552.1 31.5 %copy-start.91 = (f32[8,6912]{1,0:T(8,128)S(1)}, f32[8,6912]{1,0:T(8,128)}, u32[]{:S(2)}) copy-start(f32[8,6912]{1,0:T(8,128)} %get-tuple-element.73) | copy-start | bytes 663556
  (125 other events, 414.3 us)
Sparse Core Ops, SparseCore 0:
  10.5 50.6 all-gather.13
  62.9 34.8 all-gather.17
  100.4 51.8 all-gather.9
  154.8 30.4 all-gather.11
  187.2 63.8 all-gather.15
  252.9 63.8 all-gather.19
  420.4 50.7 reduce-scatter.38
  473.6 52.8 reduce-scatter.36
  528.8 138.6 reduce-scatter.34
  669.8 140.9 reduce-scatter.32
  813.2 181.4 reduce-scatter.46
  997.0 181.9 reduce-scatter.44
  1181.4 181.7 reduce-scatter.58
  1365.5 181.3 reduce-scatter.56
  1550.0 36.2 reduce-scatter.54
  1589.7 35.0 reduce-scatter.52
  1627.9 40.8 reduce-scatter.50
  1672.4 40.8 reduce-scatter.48
  1716.7 48.0 reduce-scatter.62
  1768.2 48.0 reduce-scatter.60
  1819.8 43.7 reduce-scatter.42
  1867.4 43.7 reduce-scatter.40
Sparse Core Ops, SparseCore 1:
  16.0 188.9 all-reduce.24
  417.4 391.0 all-reduce.22
  814.5 555.3 all-reduce.20
where the time goes:
time: 1930 us; the launch traced here: 1920 us
  waiting for transfers between devices  1500 us (78%)
  matrix products  134 us (7%)
  blocking collectives  129 us (7%)
  local copies, waits for them, and re-layouts  106 us (5%)
  other arithmetic  27.3 us (1%)
  between operations  21.9 us (1%)
    unnamed x33, waiting for transfers between devices  579 us
    reduce_scatter x2, waiting for transfers between devices, reduce_grads(): lax.psum_scatter(full_w[3].astype(jnp.bfloat16), 'fsdp', scatter_dimensio...  348 us
    psum x1, waiting for transfers between devices, ada_grads_sharded(): d_total = lax.psum(d_modulation, ('dp', 'fsdp'))  315 us
    reduce_scatter x2, waiting for transfers between devices, reduce_grads(): lax.psum_scatter(inner_sums[2].astype(jnp.bfloat16), 'dp', scatter_dimens...  92.7 us
    unnamed x328, local copies, waits for them, and re-layouts  89.1 us
    psum x1, waiting for transfers between devices, modulation_sharded(): return lax.psum(padded, ('dp', 'fsdp'))  69.7 us
    all_gather x1, waiting for transfers between devices, gather_weights(): lax.all_gather(inner_parts[3], 'dp', axis=0, tiled=True)  58.6 us
    dot_general x8, matrix products, matmul_right_t(): lax.dot_general(left, right, (((1,), (1,)), ((), ())), preferred_element_...  41 us
  transfers between devices with their start and end apart: 25, of which 16 were waited for; matrix products, arithmetic and copies ran while one was open for 9% of the time, Pallas kernels for 0%

commit v1 on v0

--- a/solution.py
+++ b/solution.py
@@ -9,6 +9,27 @@
 GELU_C = math.sqrt(2.0 / math.pi)
 PRECISE = lax.Precision.HIGHEST
 NEG_FILL = -1e30
+
+
+def collect(x, axis, dim):
+    size, index, span = (lax.axis_size(axis), lax.axis_index(axis), x.shape[dim])
+    right = [(i, (i + 1) % size) for i in range(size)]
+    backward = [(i, (i - 1) % size) for i in range(size)]
+    out = jnp.zeros((*x.shape[:dim], size * span, *x.shape[dim + 1 :]), x.dtype)
+    out = lax.dynamic_update_slice_in_dim(out, x, index * span, axis=dim)
+    from_left = from_right = x
+    half = size // 2
+    for turn in range(1, half + 1):
+        from_left = lax.ppermute(from_left, axis, right)
+        out = lax.dynamic_update_slice_in_dim(
+            out, from_left, (index - turn) % size * span, axis=dim
+        )
+        if turn < size - half:
+            from_right = lax.ppermute(from_right, axis, backward)
+            out = lax.dynamic_update_slice_in_dim(
+                out, from_right, (index + turn) % size * span, axis=dim
+            )
+    return out
 
 
 def layer_norm(values):
@@ -67,7 +88,7 @@
         lax.all_gather(inner_parts[0], "dp", axis=0, tiled=True),
         lax.all_gather(inner_parts[1], "dp", axis=0, tiled=True),
         lax.all_gather(inner_parts[2], "dp", axis=0, tiled=True),
-        lax.all_gather(inner_parts[3], "dp", axis=0, tiled=True),
+        collect(inner_parts[3], "dp", 0),
     )
     return (
         whole_rows[0],

time: 1930 us -> 2040 us (1.057)
  local copies, waits for them, and re-layouts: 106 us -> 262 us
  waiting for transfers between devices: 1500 us -> 1450 us
    dynamic_update_slice x0 -> x8, local copies, waits for them, and re-layouts: none -> 126 us  [the longest x4 62.7 us: collect(): lax.dynamic_update_slice_in_dim(out, from_left, (index - turn) % size * s...]
    ppermute x0 -> x7, waiting for transfers between devices: none -> 84.1 us  [the longest x4 54.5 us: collect(): from_left = lax.ppermute(from_left, axis, right)]
    psum x1, waiting for transfers between devices: 69.7 us -> 8.89 us  [modulation_sharded(): return lax.psum(padded, ('dp', 'fsdp'))]
    all_gather x1 -> x0, waiting for transfers between devices: 58.6 us -> none  [gather_weights(): lax.all_gather(inner_parts[3], 'dp', axis=0, tiled=True)]
    unnamed x328 -> x296, local copies, waits for them, and re-layouts: 89.1 us -> 87.5 us
    unnamed x33 -> x32, waiting for transfers between devices: 579 us -> 578 us
  transfers between devices with their start and end apart: 25 -> 31, of which waited for: 16 -> 18; matrix products, arithmetic and copies ran while one was open for 9% -> 16% of each run, Pallas kernels for 0% -> 0%
where the time goes in v1:
time: 2040 us; the launch traced here: 2030 us
  waiting for transfers between devices  1450 us (71%)
  local copies, waits for them, and re-layouts  262 us (13%)
  matrix products  129 us (6%)
  blocking collectives  129 us (6%)
  other arithmetic  25.7 us (1%)
  between operations  21.9 us (1%)
    unnamed x32, waiting for transfers between devices  578 us
    reduce_scatter x2, waiting for transfers between devices, reduce_grads(): lax.psum_scatter(full_w[3].astype(jnp.bfloat16), 'fsdp', scatter_dimensio...  346 us
    psum x1, waiting for transfers between devices, ada_grads_sharded(): d_total = lax.psum(d_modulation, ('dp', 'fsdp'))  318 us
    reduce_scatter x2, waiting for transfers between devices, reduce_grads(): lax.psum_scatter(inner_sums[2].astype(jnp.bfloat16), 'dp', scatter_dimens...  92.6 us
    unnamed x296, local copies, waits for them, and re-layouts  87.5 us
    dynamic_update_slice x4, local copies, waits for them, and re-layouts, collect(): lax.dynamic_update_slice_in_dim(out, from_left, (index - turn) % size * s...  62.7 us
    ppermute x4, waiting for transfers between devices, collect(): from_left = lax.ppermute(from_left, axis, right)  54.5 us
    dynamic_update_slice x3, local copies, waits for them, and re-layouts, collect(): lax.dynamic_update_slice_in_dim(out, from_right, (index + turn) % size *...  48.1 us
  transfers between devices with their start and end apart: 31, of which 18 were waited for; matrix products, arithmetic and copies ran while one was open for 16% of the time, Pallas kernels for 0%

profile of v1, /device:TPU:0, one launch (start us, length us, event | category | flops | bytes accessed | tf_op | source)
XLA Modules:
  0.0 2026.7 jit_solution(14908972775018451626)
XLA Ops:
  14.7 38.8 %all-gather = bf16[4,864,144]{1,2,0:T(8,128)(2,1)S(1)} all-gather(bf16[1,864,144]{1,2,0:T(8,128)(2,1)S(1)} %bitcast.249), channel_id=1, replica_groups=mesh['dp'=8,'fsdp'=4] {'fsdp'}, dimensions={0}, use_global_device_ids=true | all-gather | bytes 1244160 | tf_op jit(solution)/shard_map/all_gather | solution.py:78
  55.6 16.0 all-gather.1
  73.5 24.3 %all-gather.17.cloned.1.call-done = bf16[576,1152]{0,1:T(8,128)(2,1)} async-done(((bf16[576,288]{0,1:T(8,128)(2,1)}), bf16[576,1152]{0,1:T(8,128)(2,1)}) %all-gather.17.cloned.1.call-update) | async-done | bytes 1327120 | tf_op jit(solution)/shard_map/all_gather | solution.py:81
  103.0 40.4 %collective-permute-done = bf16[576,1152]{1,0:T(8,128)(2,1)} collective-permute-done((bf16[576,1152]{1,0:T(8,128)(2,1)}, bf16[576,1152]{1,0:T(8,128)(2,1)}, u32[]{:S(2)}, u32[]{:S(2)}) %collective-permute-start) | collective-permute-done | bytes 1327136 | tf_op jit(solution)/shard_map/ppermute | solution.py:23
  145.9 13.1 all-gather.2
  159.0 15.5 all-reduce.16
  181.2 29.6 %collective-permute-done.3 = bf16[576,1152]{1,0:T(8,128)(2,1)} collective-permute-done((bf16[576,1152]{1,0:T(8,128)(2,1)S(1)}, bf16[576,1152]{1,0:T(8,128)(2,1)}, u32[]{:S(2)}, u32[]{:S(2)}) %collective-permute-start.3) | collective-permute-done | bytes 1327136 | tf_op jit(solution)/shard_map/ppermute | solution.py:28
  213.8 9.4 collective-permute-done.4
  224.5 8.9 all-reduce.25.cloned.1.call-done
  242.6 14.8 dynamic_update_slice.45
  260.1 16.1 dynamic_update_slice.46
  278.8 16.7 dynamic_update_slice.47
  298.2 14.7 dynamic_update_slice.48
  315.5 14.8 dynamic_update_slice.49
  332.9 16.6 dynamic_update_slice.50
  352.1 16.6 dynamic_update_slice.51
  371.4 15.3 dynamic_update_slice.52
  398.7 4.7 fusion
  419.1 6.1 convolution_add_fusion.1
  425.3 6.9 fusion.139
  474.0 21.0 %all-reduce.15 = (bf16[1152]{0:T(1024)(128)(2,1)S(1)}, bf16[2304]{0:T(1024)(128)(2,1)S(1)}, bf16[2304]{0:T(1024)(128)(2,1)}, bf16[1152]{0:T(1024)(128)(2,1)}, bf...) all-reduce(bf16[1152]{0:T(1024)(128)(2,1)S(1)} %copy-done.100, ...), channel_id=1, replica_groups=mesh['dp'=8,'fsdp'=4] {'fsdp'}, use_global_device_ids=true, to_apply=%add.2 | all-reduce | flops 19584 | bytes 78336
  495.0 7.5 convolution_add_fusion.7
  502.5 7.5 convolution_add_fusion.8
  529.5 5.4 convolution_convert_fusion.4
  536.0 5.4 convolution_convert_fusion.5
  542.2 5.7 convolution_convert_fusion
  548.8 5.6 convolution_convert_fusion.1
  555.5 5.7 convolution_convert_fusion.2
  561.2 15.3 copy.170
  577.6 5.7 convolution_convert_fusion.3
  583.3 15.1 copy.168
  598.4 317.8 %all-reduce.23.cloned.1.call-done = (f32[8,6912]{1,0:T(8,128)}, f32[8,6912]{1,0:T(8,128)}) async-done(((f32[8,6912]{1,0:T(8,128)}, f32[8,6912]{1,0:T(8,128)}), (f32[8,6912]{1,0:T(8,128)}, f32[8,6912]{1,0:T(8,128)})) %all-reduce.23.cloned.1.call-update) | async-done | bytes 442384 | tf_op jit(solution)/shard_map/psum | solution.py:169
  934.0 166.4 %reduce-scatter.47.cloned.1.call-done = bf16[4608,288]{0,1:T(8,128)(2,1)} async-done(((bf16[4608,1152]{0,1:T(8,128)(2,1)}), bf16[4608,288]{0,1:T(8,128)(2,1)}) %reduce-scatter.47.cloned.1.call-update) | async-done | bytes 2654224 | tf_op jit(solution)/shard_map/reduce_scatter | solution.py:116
  1100.4 4.7 copy.174
  1105.2 179.7 %reduce-scatter.45.cloned.1.call-done = bf16[4608,288]{0,1:T(8,128)(2,1)} async-done(((bf16[4608,1152]{0,1:T(8,128)(2,1)}), bf16[4608,288]{0,1:T(8,128)(2,1)}) %reduce-scatter.45.cloned.1.call-update) | async-done | bytes 2654224 | tf_op jit(solution)/shard_map/reduce_scatter | solution.py:116
  1284.9 4.7 copy.172
  1289.6 179.3 %reduce-scatter.59.cloned.1.call-done = bf16[1152,1152]{1,0:T(8,128)(2,1)} async-done(((bf16[4608,1152]{1,0:T(8,128)(2,1)}), bf16[1152,1152]{1,0:T(8,128)(2,1)}) %reduce-scatter.59.cloned.1.call-update) | async-done | bytes 2654224
  1468.9 5.2 copy.171
  1474.2 178.6 %reduce-scatter.57.cloned.1.call-done = bf16[1152,1152]{1,0:T(8,128)(2,1)} async-done(((bf16[4608,1152]{1,0:T(8,128)(2,1)}), bf16[1152,1152]{1,0:T(8,128)(2,1)}) %reduce-scatter.57.cloned.1.call-update) | async-done | bytes 2654224
  1652.8 5.2 copy.169
  1663.2 24.7 %all-reduce.14 = (f32[576]{0:T(1024)}, f32[288]{0:T(512)}, f32[1152]{0:T(1024)}, f32[288]{0:T(512)}) all-reduce(f32[576]{0:T(1024)S(1)} %convert_add_fusion.7, f32[288]{0:T(512)S(1)} %convert_add_fusion.9, f32[1152]{0:T(1024)S(1)} %convert_add_fusion.6, f32[288]{0:T(512)S(1)} %convert_add_fusion.8), channel_id=1, replica_groups=mesh['dp'=8,'fsdp'=4] {'dp'}, use_global_device_ids=true, to_apply=%region_36.37 | all-reduce | flops 2304 | bytes 18432 | tf_op jit(solution)/shard_map/psum | solution.py:146
  1697.4 33.3 %reduce-scatter.53.cloned.1.call-done = bf16[144,288]{1,0:T(8,128)(2,1)} async-done(((bf16[1152,288]{1,0:T(8,128)(2,1)}), bf16[144,288]{1,0:T(8,128)(2,1)}) %reduce-scatter.53.cloned.1.call-update) | async-done | bytes 82960
  1732.6 42.2 %reduce-scatter.51.cloned.1.call-done = bf16[144,864]{1,0:T(8,128)(2,1)} async-done(((bf16[1152,864]{1,0:T(8,128)(2,1)}), bf16[144,864]{1,0:T(8,128)(2,1)}) %reduce-scatter.51.cloned.1.call-update) | async-done | bytes 248848
  1775.9 43.3 %reduce-scatter.49.cloned.1.call-done = bf16[144,864]{1,0:T(8,128)(2,1)} async-done(((bf16[1152,864]{1,0:T(8,128)(2,1)}), bf16[144,864]{1,0:T(8,128)(2,1)}) %reduce-scatter.49.cloned.1.call-update) | async-done | bytes 248848
  1821.5 49.1 %reduce-scatter.63.cloned.1.call-done = bf16[576,288]{1,0:T(8,128)(2,1)} async-done(((bf16[4608,288]{1,0:T(8,128)(2,1)}), bf16[576,288]{1,0:T(8,128)(2,1)}) %reduce-scatter.63.cloned.1.call-update) | async-done | bytes 331792
  1871.8 50.4 %reduce-scatter.61.cloned.1.call-done = bf16[576,288]{1,0:T(8,128)(2,1)} async-done(((bf16[4608,288]{1,0:T(8,128)(2,1)}), bf16[576,288]{1,0:T(8,128)(2,1)}) %reduce-scatter.61.cloned.1.call-update) | async-done | bytes 331792
  1924.4 44.9 %reduce-scatter.43.cloned.1.call-done = bf16[144,1152]{1,0:T(8,128)(2,1)} async-done(((bf16[1152,1152]{1,0:T(8,128)(2,1)}), bf16[144,1152]{1,0:T(8,128)(2,1)}) %reduce-scatter.43.cloned.1.call-update) | async-done | bytes 331792 | tf_op jit(solution)/shard_map/reduce_scatter | solution.py:139
  1969.3 47.7 %reduce-scatter.41.cloned.1.call-done = bf16[144,1152]{1,0:T(8,128)(2,1)} async-done(((bf16[1152,1152]{1,0:T(8,128)(2,1)}), bf16[144,1152]{1,0:T(8,128)(2,1)}) %reduce-scatter.41.cloned.1.call-update) | async-done | bytes 331792 | tf_op jit(solution)/shard_map/reduce_scatter | solution.py:139
  (520 shorter events, 188.7 us)
Async XLA Ops:
  8.0 64.9 %all-gather.13.cloned.1.call-start = ((), (), s32[]{:S(2)}) async-start(), calls=%async_computation.18 | async-start | bytes 1658880 | tf_op jit(solution)/shard_map/all_gather | solution.py:80
  8.8 89.0 %all-gather.17.cloned.1.call-start = ((), (), s32[]{:S(2)}) async-start(), calls=%async_computation.20 | async-start | bytes 1843200 | tf_op jit(solution)/shard_map/all_gather | solution.py:81
  9.5 223.9 %all-reduce.25.cloned.1.call-start = ((), (), s32[]{:S(2)}) async-start(), calls=%async_computation.39 | async-start | bytes 884736 | tf_op jit(solution)/shard_map/psum | solution.py:162
  14.6 372.1 %all-gather.9.cloned.1.call-start = ((), (), s32[]{:S(2)}) async-start(), calls=%async_computation.16 | async-start | bytes 8957952 | tf_op jit(solution)/shard_map/all_gather | solution.py:88
  55.6 355.8 %all-gather.11.cloned.1.call-start = ((), (), s32[]{:S(2)}) async-start(), calls=%async_computation.17 | async-start | bytes 2985984 | tf_op jit(solution)/shard_map/all_gather | solution.py:89
  72.8 346.3 %all-gather.15.cloned.1.call-start = ((), (), s32[]{:S(2)}) async-start(), calls=%async_computation.19 | async-start | bytes 11943936 | tf_op jit(solution)/shard_map/all_gather | solution.py:90
  72.9 70.5 %copy-start.110 = (u32[32]{0:T(128)S(1)}, u32[32]{0:T(128)}, u32[]{:S(2)}) copy-start(u32[32]{0:T(128)} %constant.154) | copy-start | bytes 388
  72.9 72.4 %copy-start.109 = (bf16[1152]{0:T(1024)(128)(2,1)S(1)}, bf16[1152]{0:T(1024)(128)(2,1)}, u32[]{:S(2)}) copy-start(bf16[1152]{0:T(1024)(128)(2,1)} %param.27) | copy-start | bytes 6916
  72.9 72.4 %copy-start.111 = (bf16[576]{0:T(1024)(128)(2,1)S(1)}, bf16[576]{0:T(1024)(128)(2,1)}, u32[]{:S(2)}) copy-start(bf16[576]{0:T(1024)(128)(2,1)} %param.23) | copy-start | bytes 3460
  72.9 72.7 %copy-start.116 = (bf16[288]{0:T(512)(128)(2,1)S(1)}, bf16[288]{0:T(512)(128)(2,1)}, u32[]{:S(2)}) copy-start(bf16[288]{0:T(512)(128)(2,1)} %param.25) | copy-start | bytes 1732
  73.4 101.1 %copy-start.18 = (bf16[2,64,1152]{2,1,0:T(8,128)(2,1)S(1)}, bf16[2,64,1152]{2,1,0:T(8,128)(2,1)}, u32[]{:S(2)}) copy-start(bf16[2,64,1152]{2,1,0:T(8,128)(2,1)} %param.15) | copy-start | bytes 884740
  73.4 106.4 %copy-start.117 = (s32[2,64]{1,0:T(2,128)S(1)}, s32[2,64]{1,0:T(2,128)}, u32[]{:S(2)}) copy-start(s32[2,64]{1,0:T(2,128)} %param.19) | copy-start | bytes 1540
  73.4 106.4 %copy-start.118 = (s32[2,64]{1,0:T(2,128)S(1)}, s32[2,64]{1,0:T(2,128)}, u32[]{:S(2)}) copy-start(s32[2,64]{1,0:T(2,128)} %param.18) | copy-start | bytes 1540
  73.5 150.8 %copy-start.119 = (bf16[288]{0:T(512)(128)(2,1)S(1)}, bf16[288]{0:T(512)(128)(2,1)}, u32[]{:S(2)}) copy-start(bf16[288]{0:T(512)(128)(2,1)} %param.29) | copy-start | bytes 1732
  73.5 842.8 %all-reduce.23.cloned.1.call-start = ((), (), s32[]{:S(2)}) async-start(), calls=%async_computation.38 | async-start | bytes 884736 | tf_op jit(solution)/shard_map/psum | solution.py:169
  100.4 43.0 %collective-permute-start = (bf16[576,1152]{1,0:T(8,128)(2,1)}, bf16[576,1152]{1,0:T(8,128)(2,1)}, u32[]{:S(2)}, u32[]{:S(2)}) collective-permute-start(bf16[576,1152]{1,0:T(8,128)(2,1)} %copy.122), channel_id=1, source_target_pairs={{0,4},{4,8},{8,12},{12,16},{16,20},{20,24},{24,28},{28,0},{1,5},{5... | collective-permute-start | bytes 3981320 | tf_op jit(solution)/shard_map/ppermute | solution.py:23
  100.4 74.7 %collective-permute-start.1 = (bf16[576,1152]{1,0:T(8,128)(2,1)}, bf16[576,1152]{1,0:T(8,128)(2,1)S(1)}, u32[]{:S(2)}, u32[]{:S(2)}) collective-permute-start(bf16[576,1152]{1,0:T(8,128)(2,1)} %copy.122), channel_id=1, source_target_pairs={{0,28},{4,0},{8,4},{12,8},{16,12},{20,16},{24,20},{28,24},{1,29},{... | collective-permute-start | bytes 3981320 | tf_op jit(solution)/shard_map/ppermute | solution.py:28
  143.4 36.4 %collective-permute-start.2 = (bf16[576,1152]{1,0:T(8,128)(2,1)}, bf16[576,1152]{1,0:T(8,128)(2,1)}, u32[]{:S(2)}, u32[]{:S(2)}) collective-permute-start(bf16[576,1152]{1,0:T(8,128)(2,1)} %collective-permute-done), channel_id=1, source_target_pairs={{0,4},{4,8},{8,12},{12,16},{16,20},{20,24},{24,28},{28,0},{1,5},{5... | collective-permute-start | bytes 3981320 | tf_op jit(solution)/shard_map/ppermute | solution.py:23
  174.7 63.0 %copy-start.101 = (f32[64]{0:T(128)}, f32[64]{0:T(128)S(1)}, u32[]{:S(2)}) copy-start(f32[64]{0:T(128)S(1)} %broadcast_multiply_fusion.3) | copy-start | bytes 772
  174.7 63.0 %copy-start.103 = (f32[64]{0:T(128)}, f32[64]{0:T(128)S(1)}, u32[]{:S(2)}) copy-start(f32[64]{0:T(128)S(1)} %broadcast_multiply_fusion.1) | copy-start | bytes 772
  175.0 62.7 %copy-start.112 = (f32[64]{0:T(128)}, f32[64]{0:T(128)S(1)}, u32[]{:S(2)}) copy-start(f32[64]{0:T(128)S(1)} %fusion.129) | copy-start | bytes 772
  175.0 58.3 %copy-start.56 = (bf16[576,1152]{1,0:T(8,128)(2,1)}, bf16[576,1152]{1,0:T(8,128)(2,1)S(1)}, u32[]{:S(2)}) copy-start(bf16[576,1152]{1,0:T(8,128)(2,1)S(1)} %collective-permute-done.1) | copy-start | bytes 3981316
  175.1 35.8 %collective-permute-start.3 = (bf16[576,1152]{1,0:T(8,128)(2,1)S(1)}, bf16[576,1152]{1,0:T(8,128)(2,1)}, u32[]{:S(2)}, u32[]{:S(2)}) collective-permute-start(bf16[576,1152]{1,0:T(8,128)(2,1)S(1)} %collective-permute-done.1), channel_id=1, source_target_pairs={{0,28},{4,0},{8,4},{12,8},{16,12},{20,16},{24,20},{28,24},{1,29},{... | collective-permute-start | bytes 3981320 | tf_op jit(solution)/shard_map/ppermute | solution.py:28
  179.8 43.4 %collective-permute-start.4 = (bf16[576,1152]{1,0:T(8,128)(2,1)}, bf16[576,1152]{1,0:T(8,128)(2,1)}, u32[]{:S(2)}, u32[]{:S(2)}) collective-permute-start(bf16[576,1152]{1,0:T(8,128)(2,1)} %collective-permute-done.2), channel_id=1, source_target_pairs={{0,4},{4,8},{8,12},{12,16},{16,20},{20,24},{24,28},{28,0},{1,5},{5... | collective-permute-start | bytes 3981320 | tf_op jit(solution)/shard_map/ppermute | solution.py:23
  179.8 57.9 %copy-start.114 = (f32[64]{0:T(128)}, f32[64]{0:T(128)S(1)}, u32[]{:S(2)}) copy-start(f32[64]{0:T(128)S(1)} %fusion.131) | copy-start | bytes 772
  210.8 138.7 %collective-permute-start.5 = (bf16[576,1152]{1,0:T(8,128)(2,1)}, bf16[576,1152]{1,0:T(8,128)(2,1)}, u32[]{:S(2)}, u32[]{:S(2)}) collective-permute-start(bf16[576,1152]{1,0:T(8,128)(2,1)} %collective-permute-done.3), channel_id=1, source_target_pairs={{0,28},{4,0},{8,4},{12,8},{16,12},{20,16},{24,20},{28,24},{1,29},{... | collective-permute-start | bytes 3981320 | tf_op jit(solution)/shard_map/ppermute | solution.py:28
  223.2 145.6 %collective-permute-start.6 = (bf16[576,1152]{1,0:T(8,128)(2,1)}, bf16[576,1152]{1,0:T(8,128)(2,1)}, u32[]{:S(2)}, u32[]{:S(2)}) collective-permute-start(bf16[576,1152]{1,0:T(8,128)(2,1)} %collective-permute-done.4), channel_id=1, source_target_pairs={{0,4},{4,8},{8,12},{12,16},{16,20},{20,24},{24,28},{28,0},{1,5},{5... | collective-permute-start | bytes 3981320 | tf_op jit(solution)/shard_map/ppermute | solution.py:23
  223.5 163.2 %copy-start.84 = (f32[3456]{0:T(1024)}, f32[3456]{0:T(1024)S(1)}, u32[]{:S(2)}) copy-start(f32[3456]{0:T(1024)S(1)} %maximum_convert_fusion) | copy-start | bytes 41476
  235.3 197.0 %copy-start.3 = (f32[64,6912]{1,0:T(8,128)}, f32[64,6912]{1,0:T(8,128)S(1)}, u32[]{:S(2)}) copy-start(f32[64,6912]{1,0:T(8,128)S(1)} %fusion.108) | copy-start | bytes 5308420
  238.0 148.7 %copy-start.41 = (bf16[64,1152]{1,0:T(8,128)(2,1)}, bf16[64,1152]{1,0:T(8,128)(2,1)S(1)}, u32[]{:S(2)}) copy-start(bf16[64,1152]{1,0:T(8,128)(2,1)S(1)} %get-tuple-element.140) | copy-start | bytes 442372
  238.0 160.7 %copy-start.39 = (bf16[64,1152]{1,0:T(8,128)(2,1)}, bf16[64,1152]{1,0:T(8,128)(2,1)S(1)}, u32[]{:S(2)}) copy-start(bf16[64,1152]{1,0:T(8,128)(2,1)S(1)} %get-tuple-element.139) | copy-start | bytes 442372
  522.4 397.9 %reduce-scatter.39.cloned.1.call-start = ((), (), s32[]{:S(2)}) async-start(), calls=%async_computation.24 | async-start | bytes 3317760 | tf_op jit(solution)/shard_map/reduce_scatter | solution.py:110
  525.1 397.9 %reduce-scatter.37.cloned.1.call-start = ((), (), s32[]{:S(2)}) async-start(), calls=%async_computation.23 | async-start | bytes 3317760 | tf_op jit(solution)/shard_map/reduce_scatter | solution.py:110
  528.5 397.0 %reduce-scatter.35.cloned.1.call-start = ((), (), s32[]{:S(2)}) async-start(), calls=%async_computation.22 | async-start | bytes 9953280 | tf_op jit(solution)/shard_map/reduce_scatter | solution.py:107
  534.9 394.8 %reduce-scatter.33.cloned.1.call-start = ((), (), s32[]{:S(2)}) async-start(), calls=%async_computation.21 | async-start | bytes 9953280 | tf_op jit(solution)/shard_map/reduce_scatter | solution.py:107
  541.4 559.0 %reduce-scatter.47.cloned.1.call-start = ((), (), s32[]{:S(2)}) async-start(), calls=%async_computation.28 | async-start | bytes 13271040 | tf_op jit(solution)/shard_map/reduce_scatter | solution.py:116
  548.0 736.9 %reduce-scatter.45.cloned.1.call-start = ((), (), s32[]{:S(2)}) async-start(), calls=%async_computation.27 | async-start | bytes 13271040 | tf_op jit(solution)/shard_map/reduce_scatter | solution.py:116
  554.4 914.5 %reduce-scatter.59.cloned.1.call-start = ((), (), s32[]{:S(2)}) async-start(), calls=%async_computation.34 | async-start | bytes 13271040
  576.5 1076.3 %reduce-scatter.57.cloned.1.call-start = ((), (), s32[]{:S(2)}) async-start(), calls=%async_computation.33 | async-start | bytes 13271040
  598.4 1095.8 %all-reduce.21.cloned.1.call-start = ((), (), s32[]{:S(2)}) async-start(), calls=%async_computation.37 | async-start | bytes 147456 | tf_op jit(solution)/shard_map/psum | solution.py:178
  920.3 776.1 %reduce-scatter.55.cloned.1.call-start = ((), (), s32[]{:S(2)}) async-start(), calls=%async_computation.32 | async-start | bytes 995328
  922.8 807.9 %reduce-scatter.53.cloned.1.call-start = ((), (), s32[]{:S(2)}) async-start(), calls=%async_computation.31 | async-start | bytes 995328
  925.4 849.4 %reduce-scatter.51.cloned.1.call-start = ((), (), s32[]{:S(2)}) async-start(), calls=%async_computation.30 | async-start | bytes 2322432
  929.7 889.4 %reduce-scatter.49.cloned.1.call-start = ((), (), s32[]{:S(2)}) async-start(), calls=%async_computation.29 | async-start | bytes 2322432
  933.9 936.7 %reduce-scatter.63.cloned.1.call-start = ((), (), s32[]{:S(2)}) async-start(), calls=%async_computation.36 | async-start | bytes 3981312
  1105.1 817.1 %reduce-scatter.61.cloned.1.call-start = ((), (), s32[]{:S(2)}) async-start(), calls=%async_computation.35 | async-start | bytes 3981312
  1289.6 679.7 %reduce-scatter.43.cloned.1.call-start = ((), (), s32[]{:S(2)}) async-start(), calls=%async_computation.26 | async-start | bytes 2985984 | tf_op jit(solution)/shard_map/reduce_scatter | solution.py:139
  1474.1 542.8 %reduce-scatter.41.cloned.1.call-start = ((), (), s32[]{:S(2)}) async-start(), calls=%async_computation.25 | async-start | bytes 2985984 | tf_op jit(solution)/shard_map/reduce_scatter | solution.py:139
  (115 other events, 767.4 us)
Sparse Core Ops, SparseCore 0:
  10.5 50.6 all-gather.12
  62.8 34.9 all-gather.16
  100.4 73.5 all-gather.8
  176.5 40.2 all-gather.10
  218.7 78.3 all-gather.14
  525.3 51.8 reduce-scatter.38
  579.5 52.7 reduce-scatter.36
  634.6 138.6 reduce-scatter.34
  775.8 140.8 reduce-scatter.32
  918.9 181.4 reduce-scatter.46
  1102.8 181.9 reduce-scatter.44
  1287.1 181.7 reduce-scatter.58
  1471.3 181.3 reduce-scatter.56
  1655.9 36.2 reduce-scatter.54
  1695.6 35.0 reduce-scatter.52
  1733.9 40.7 reduce-scatter.50
  1778.3 40.7 reduce-scatter.48
  1822.5 48.0 reduce-scatter.62
  1874.1 48.0 reduce-scatter.60
  1925.5 43.7 reduce-scatter.42
  1973.2 43.7 reduce-scatter.40
Sparse Core Ops, SparseCore 1:
  16.0 217.4 all-reduce.24
  522.5 393.7 all-reduce.22
  922.4 553.2 all-reduce.20
